TPU v7x, 256 devices: a whole 4x4x8 slice. The times are simulated.
256 devices in a mesh: rep: 32 (over z_lo, x, core), fsdp: 8 (over y, z_hi).
Axes of the slice: x: 4, y: 4, z: 8 (z_hi: 2, z_lo: 4; z = z_hi * 4 + z_lo), core: 2. Of those that a mesh axis runs over, the one named last changes fastest.
Arguments:
- global_weights: bfloat16 [8192, 1024], P(None, 'fsdp'), may hold values from -0.75 to 0.75
- momentum: float32 [8192, 1024], P('rep', 'fsdp'), may hold values from -0.3125 to 0.3125
- first_moment: float32 [32, 8192, 1024], P('rep', None, 'fsdp'), may hold values from -0.0029296875 to 0.0029296875
- second_moment: float32 [32, 8192, 1024], P('rep', None, 'fsdp'), may hold values from 1e-08 to 1e-07
- hidden_bank: bfloat16 [32, 256, 8192], P('rep', 'fsdp'), may hold values from -0.15625 to 0.15625
- target_bank: bfloat16 [32, 256, 1024], P('rep', None, 'fsdp'), may hold values from -6 to 6
- token_ids: int32 [32, 2, 512], P('rep'), may hold values from 0 to 255
Outputs:
- new_weights: bfloat16 [8192, 1024], P(None, 'fsdp')
- new_momentum: float32 [8192, 1024], P('rep', 'fsdp')
All inputs are finite; a program needn't handle non-finite values.
Results may differ from a plain program's by a relative error of at most 0.0034.
Values may be sent and summed in bfloat16 or wider, within the bound.
A program may use at most 128 MiB of HBM per device.

v0:
```python
import jax
import jax.numpy as jnp
from jax import lax
from jax.sharding import PartitionSpec as P


def per_device(
    global_weights, momentum, first_moment, second_moment, hidden_bank, target_bank, token_ids
):
    ids_all = token_ids[0]
    inner_count = ids_all.shape[0]
    token_count = ids_all.shape[1]
    flat_ids = ids_all.reshape(-1)
    local_bank = hidden_bank[0]
    whole_bank = lax.all_gather(local_bank, "fsdp", axis=0, tiled=True)
    picked_all = jnp.take(whole_bank, flat_ids, axis=0)
    picked_all = picked_all.reshape(inner_count, token_count, local_bank.shape[1])
    targets = target_bank[0]
    start_weights = global_weights.astype(jnp.float32)
    weights = start_weights
    first_state = first_moment[0]
    second_state = second_moment[0]
    for inner_step in range(inner_count):
        picked = picked_all[inner_step]
        wanted = jnp.take(targets, ids_all[inner_step], axis=0)
        output = jnp.dot(picked, weights.astype(jnp.bfloat16), preferred_element_type=jnp.float32)
        residual_out = ((output - wanted.astype(jnp.float32)) / token_count).astype(jnp.bfloat16)
        gradient = lax.dot_general(
            picked, residual_out, (((0,), (0,)), ((), ())), preferred_element_type=jnp.float32
        )
        first_state = 0.9 * first_state + 0.1 * gradient
        second_state = 0.95 * second_state + 0.05 * gradient * gradient
        weights = weights - 0.1 * (first_state / (jnp.sqrt(second_state) + 1e-08) + 0.1 * weights)
    local_change = start_weights - weights
    share_rows = momentum.shape[0]
    row_begin = lax.axis_index("rep") * share_rows
    full_momentum = lax.all_gather(momentum, "rep", axis=0, tiled=True)
    summed = lax.psum(local_change, "rep")
    average = summed / lax.axis_size("rep")
    full_new = 0.9 * full_momentum + average
    new_weights = (start_weights - 0.7 * (average + 0.9 * full_new)).astype(jnp.bfloat16)
    new_momentum = lax.dynamic_slice_in_dim(full_new, row_begin, share_rows, 0)
    return (new_weights, new_momentum)


def solution(mesh):
    return jax.shard_map(
        per_device,
        mesh=mesh,
        in_specs=(
            P(None, "fsdp"),
            P("rep", "fsdp"),
            P("rep", None, "fsdp"),
            P("rep", None, "fsdp"),
            P("rep", "fsdp", None),
            P("rep", None, "fsdp"),
            P("rep", None, None),
        ),
        out_specs=(P(None, "fsdp"), P("rep", "fsdp")),
        check_vma=False,
    )
```

profile of v0, /device:TPU:1, one launch (start us, length us, event | category | flops | bytes accessed | tf_op | source)
XLA Modules:
  0.0 484.0 jit_solution(12017443825322824904)
XLA Ops:
  7.2 0.0 copy-start
  7.2 0.0 all-gather.6.cloned.1.call-start
  7.2 0.7 all-gather.6.cloned.1.call-update
  7.9 0.0 all-gather.4.cloned.1.call-start
  8.0 0.7 all-gather.4.cloned.1.call-update
  8.7 0.0 all-reduce.2.cloned.1.call-start
  8.7 0.8 fusion.55
  9.5 0.7 copy.10
  10.2 0.7 copy.9
  11.0 0.0 copy-done
  11.0 1.3 gather_fusion.1
  12.3 1.3 gather_fusion.2
  13.7 107.5 %all-gather.6.cloned.1.call-done = bf16[1,256,8192]{2,1,0:T(8,128)(2,1)} async-done(((bf16[1,32,8192]{2,1,0:T(8,128)(2,1)}), bf16[1,256,8192]{2,1,0:T(8,128)(2,1)}) %all-gather.6.cloned.1.call-update) | async-done | bytes 4194320 | tf_op jit(solution)/shard_map/all_gather | solution.py:15
  121.1 30.6 %gather_fusion = bf16[1024,8192]{1,0:T(8,128)(2,1)} fusion(bf16[256,8192]{1,0:T(8,128)(2,1)} %bitcast.35, s32[1024]{0:T(1024)S(1)} %broadcast_clamp_fusion), kind=kCustom, calls=%fused_computation.2 | custom fusion | bytes 33558528 | tf_op jit(solution)/shard_map/jit(_take)/gather | solution.py:16
  151.7 0.0 copy-start.2
  151.7 8.8 %broadcast_select_fusion = bf16[1024,8192]{1,0:T(8,128)(2,1)S(1)} fusion(bf16[1024,8192]{1,0:T(8,128)(2,1)} %gather_fusion, pred[1024]{0:T(1024)(128)(4,1)S(1)} %compare_and_fusion), kind=kLoop, calls=%fused_computation.3 | loop fusion | flops 8388608 | bytes 33555456 | tf_op jit(solution)/shard_map/jit(_take)/select_n | solution.py:16
  160.6 0.0 copy-done.2
  160.6 2.4 fusion.31
  162.9 4.3 fusion.4
  167.3 7.6 %fusion.44 = bf16[512,128]{1,0:T(8,128)(2,1)S(1)} fusion(bf16[8192,128]{1,0:T(8,128)(2,1)S(1)} %copy-done.2, f32[8192,128]{1,0:T(8,128)} %fusion.4, f32[1,8192,128]{2,1,0:T(8,128)} %param.11, bf16[1024,8192]{1,0:T(8,128)(2,1)S(1)} %broadcast_select_fusion, f32[1,8192,128]{2,1,0:T(8,128)} %param.12, bf16[512,128]{1,0:T(8,128)(2,1)S(1)} %gather_fusion.2, ...), kind=kOutput, calls=%fused_computation.39 | convolution fusion | flops 1089798144 | bytes 23331328 | tf_op jit(solution)/shard_map/dot_general | solution.py:26
  174.9 11.2 %convert_subtract_fusion.1 = f32[8192,128]{1,0:T(8,128)} fusion(bf16[8192,128]{1,0:T(8,128)(2,1)S(1)} %copy-done.2, bf16[512,128]{1,0:T(8,128)(2,1)S(1)} %fusion.44, bf16[1024,8192]{1,0:T(8,128)(2,1)S(1)} %broadcast_select_fusion, f32[8192,128]{1,0:T(8,128)} %fusion.4, f32[1,8192,128]{2,1,0:T(8,128)} %param.11, f32[1,8192,128]{2,1,0:T(8,128)} %param.12), kind=kOutput, calls=%fused_computation.13 | convolution fusion | flops 1103101952 | bytes 27394048 | tf_op jit(solution)/shard_map/dot_general | solution.py:28
  186.1 0.0 all-reduce.2.cloned.1.call-update
  186.1 0.0 all-gather.4.cloned.1.call-done
  186.1 284.6 %all-reduce.2.cloned.1.call-done = f32[8192,128]{1,0:T(8,128)} async-done(((f32[8192,128]{1,0:T(8,128)}), f32[8192,128]{1,0:T(8,128)}) %all-reduce.2.cloned.1.call-update) | async-done | bytes 4194320 | tf_op jit(solution)/shard_map/psum | solution.py:38
  470.7 0.0 copy-start.1
  470.8 6.0 %multiply_add_fusion = (f32[8192,128]{1,0:T(8,128)S(1)}, bf16[8192,128]{1,0:T(8,128)(2,1)}) fusion(f32[8192,128]{1,0:T(8,128)} %all-gather.4.cloned.1.call-done, f32[8192,128]{1,0:T(8,128)} %all-reduce.2.cloned.1.call-done, bf16[8192,128]{1,0:T(8,128)(2,1)S(1)} %copy-done.2), kind=kLoop, calls=%fused_computation.30 | loop fusion | flops 9437184 | bytes 16777216 | tf_op jit(solution)/shard_map/add | solution.py:40
  476.8 0.7 constant_dynamic-slice_fusion
  477.4 0.0 copy-done.1
  (9 shorter events, 0.1 us)
Async XLA Ops:
  7.2 3.8 copy-start
  7.2 114.0 %all-gather.6.cloned.1.call-start = ((), (), s32[]{:S(2)}) async-start(), calls=%async_computation.2 | async-start | bytes 4718592 | tf_op jit(solution)/shard_map/all_gather | solution.py:15
  7.9 178.2 %all-gather.4.cloned.1.call-start = ((), (), s32[]{:S(2)}) async-start(), calls=%async_computation.1 | async-start | bytes 4325376 | tf_op jit(solution)/shard_map/all_gather | solution.py:37
  8.7 462.1 %all-reduce.2.cloned.1.call-start = ((), (), s32[]{:S(2)}) async-start(), calls=%async_computation | async-start | bytes 8388608 | tf_op jit(solution)/shard_map/psum | solution.py:38
  151.7 8.8 %copy-start.2 = (bf16[8192,128]{1,0:T(8,128)(2,1)S(1)}, bf16[8192,128]{1,0:T(8,128)(2,1)}, u32[]{:S(2)}) copy-start(bf16[8192,128]{1,0:T(8,128)(2,1)} %param.9) | copy-start | bytes 6291460
  470.7 6.7 %copy-start.1 = (bf16[1,256,128]{2,1,0:T(8,128)(2,1)S(1)}, bf16[1,256,128]{2,1,0:T(8,128)(2,1)}, u32[]{:S(2)}) copy-start(bf16[1,256,128]{2,1,0:T(8,128)(2,1)} %param.14) | copy-start | bytes 196612
Sparse Core Ops, SparseCore 0:
  10.6 110.4 all-gather.5
  123.0 58.3 all-gather.3
  186.2 284.4 all-reduce.1
where the time goes:
time: 484 us
  waiting for transfers between devices  394 us (81%)
  local copies, waits for them, and re-layouts  36.1 us (7%)
  matrix products  25.5 us (5%)
  other arithmetic  14.9 us (3%)
  between operations  13.9 us (3%)
    psum x1, waiting for transfers between devices, per_device(): summed = lax.psum(local_change, 'rep')  285 us
    all_gather x1, waiting for transfers between devices, per_device(): whole_bank = lax.all_gather(local_bank, 'fsdp', axis=0, tiled=True)  107 us
    gather x1, local copies, waits for them, and re-layouts, per_device(): picked_all = jnp.take(whole_bank, flat_ids, axis=0)  30.6 us
    dot_general x2, matrix products, per_device(): lax.dot_general(picked, residual_out, (((0,), (0,)), ((), ())), preferred...  15.5 us
    dot_general x2, matrix products, per_device(): jnp.dot(picked, weights.astype(jnp.bfloat16), preferred_element_type=jnp....  9.95 us
  transfers between devices with their start and end apart: 3, of which 2 were waited for; matrix products, arithmetic and copies ran while one was open for 14% of the time, Pallas kernels for 0%

commit v1 on v0

v1 whole, which is shorter than its diff:
```python
import jax
import jax.numpy as jnp
from jax import lax
from jax.sharding import PartitionSpec as P


def per_device(
    global_weights, momentum, first_moment, second_moment, hidden_bank, target_bank, token_ids
):
    ids_all = token_ids[0]
    inner_count, token_count = ids_all.shape
    bank = lax.all_gather(hidden_bank[0], "fsdp", axis=0, tiled=True)
    store = bank.shape[0]
    targets = target_bank[0].astype(jnp.float32)
    counts = (ids_all[:, None, :] == jnp.arange(store, dtype=jnp.int32)[None, :, None]).astype(
        jnp.float32
    ).sum(axis=2)
    start_weights = global_weights.astype(jnp.float32)
    weights = start_weights
    first_state = first_moment[0]
    second_state = second_moment[0]
    for inner_step in range(inner_count):
        output = jnp.dot(bank, weights.astype(jnp.bfloat16), preferred_element_type=jnp.float32)
        residual = ((output - targets) / token_count).astype(jnp.bfloat16).astype(jnp.float32)
        scaled = (residual * counts[inner_step][:, None]).astype(jnp.bfloat16)
        gradient = lax.dot_general(
            bank, scaled, (((0,), (0,)), ((), ())), preferred_element_type=jnp.float32
        )
        first_state = 0.9 * first_state + 0.1 * gradient
        second_state = 0.95 * second_state + 0.05 * gradient * gradient
        weights = weights - 0.1 * (first_state / (jnp.sqrt(second_state) + 1e-08) + 0.1 * weights)
    local_change = start_weights - weights
    share_rows = momentum.shape[0]
    row_begin = lax.axis_index("rep") * share_rows
    summed = lax.psum_scatter(local_change, "rep", scatter_dimension=0, tiled=True)
    average = summed / lax.axis_size("rep")
    new_momentum = 0.9 * momentum + average
    start_share = lax.dynamic_slice_in_dim(start_weights, row_begin, share_rows, 0)
    new_share = (start_share - 0.7 * (average + 0.9 * new_momentum)).astype(jnp.bfloat16)
    new_weights = lax.all_gather(new_share, "rep", axis=0, tiled=True)
    return (new_weights, new_momentum)


def solution(mesh):
    return jax.shard_map(
        per_device,
        mesh=mesh,
        in_specs=(
            P(None, "fsdp"),
            P("rep", "fsdp"),
            P("rep", None, "fsdp"),
            P("rep", None, "fsdp"),
            P("rep", "fsdp", None),
            P("rep", None, "fsdp"),
            P("rep", None, None),
        ),
        out_specs=(P(None, "fsdp"), P("rep", "fsdp")),
        check_vma=False,
    )
```

time: 484 us -> 368 us (0.76)
  waiting for transfers between devices: 394 us -> 303 us
  local copies, waits for them, and re-layouts: 36.1 us -> 19.5 us
  other arithmetic: 14.9 us -> 4.2 us
    psum x1 -> x0, waiting for transfers between devices: 285 us -> none  [per_device(): summed = lax.psum(local_change, 'rep')]
    reduce_scatter x0 -> x1, waiting for transfers between devices: none -> 138 us  [per_device(): lax.psum_scatter(local_change, 'rep', scatter_dimension=0, tiled=True)]
    all_gather x2, waiting for transfers between devices: 108 us -> 165 us  [the longest x1 98.8 us: per_device(): bank = lax.all_gather(hidden_bank[0], 'fsdp', axis=0, tiled=True)]
    gather x3 -> x0, local copies, waits for them, and re-layouts: 33.3 us -> none  [the longest x1 30.6 us: per_device(): picked_all = jnp.take(whole_bank, flat_ids, axis=0)]
    unnamed x8 -> x20, local copies, waits for them, and re-layouts: 1.4 us -> 19.5 us
    select_n x4 -> x0, other arithmetic: 8.82 us -> none  [the longest x2 8.82 us: per_device(): picked_all = jnp.take(whole_bank, flat_ids, axis=0)]
    dot_general x4 -> x3, matrix products: 25.5 us -> 26.3 us  [the longest x2 16 us: per_device(): lax.dot_general(bank, scaled, (((0,), (0,)), ((), ())), preferred_element...]
  transfers between devices with their start and end apart: 3 -> 3, of which waited for: 2 -> 3; matrix products, arithmetic and copies ran while one was open for 14% -> 5% of each run, Pallas kernels for 0% -> 0%
where the time goes in v1:
time: 368 us; the launch traced here: 367 us
  waiting for transfers between devices  303 us (82%)
  matrix products  26.3 us (7%)
  local copies, waits for them, and re-layouts  19.5 us (5%)
  between operations  13.8 us (4%)
  other arithmetic  4.2 us (1%)
    reduce_scatter x1, waiting for transfers between devices, per_device(): lax.psum_scatter(local_change, 'rep', scatter_dimension=0, tiled=True)  138 us
    all_gather x1, waiting for transfers between devices, per_device(): bank = lax.all_gather(hidden_bank[0], 'fsdp', axis=0, tiled=True)  98.8 us
    all_gather x1, waiting for transfers between devices, per_device(): new_weights = lax.all_gather(new_share, 'rep', axis=0, tiled=True)  65.8 us
    unnamed x20, local copies, waits for them, and re-layouts  19.5 us
    dot_general x2, matrix products, per_device(): lax.dot_general(bank, scaled, (((0,), (0,)), ((), ())), preferred_element...  16 us
    dot_general x1, matrix products, per_device(): jnp.dot(bank, weights.astype(jnp.bfloat16), preferred_element_type=jnp.fl...  10.3 us
  transfers between devices with their start and end apart: 3, of which 3 were waited for; matrix products, arithmetic and copies ran while one was open for 5% of the time, Pallas kernels for 0%

profile of v1, /device:TPU:1, one launch (start us, length us, event | category | flops | bytes accessed | tf_op | source)
XLA Modules:
  0.0 367.2 jit_solution(17485221582282714462)
XLA Ops:
  7.2 0.0 all-gather.6.cloned.1.call-start
  7.2 0.7 all-gather.6.cloned.1.call-update
  7.9 0.0 reduce-scatter.2.cloned.1.call-start
  7.9 2.9 copy.15
  10.9 5.6 %copy.16 = f32[1,8192,128]{1,2,0:T(8,128)} copy(f32[1,8192,128]{2,1,0:T(8,128)} %param.9) | data formatting | bytes 8388608 | tf_op args[2]
  16.5 0.0 copy-start.6
  16.5 0.0 copy-start.5
  16.5 5.7 %copy.17 = f32[1,8192,128]{1,2,0:T(8,128)} copy(f32[1,8192,128]{2,1,0:T(8,128)} %param.10) | data formatting | bytes 8388608 | tf_op args[3]
  22.2 0.0 copy-done.6
  22.2 0.2 convert_reduce_fusion
  22.4 98.8 %all-gather.6.cloned.1.call-done = bf16[1,256,8192]{2,1,0:T(8,128)(2,1)} async-done(((bf16[1,32,8192]{2,1,0:T(8,128)(2,1)}), bf16[1,256,8192]{2,1,0:T(8,128)(2,1)}) %all-gather.6.cloned.1.call-update) | async-done | bytes 4194320 | tf_op jit(solution)/shard_map/all_gather | solution.py:12
  121.2 0.0 copy-done.5
  121.2 8.0 %convolution_bitcast_fusion.1 = f32[8192,128]{0,1:T(8,128)} fusion(bf16[1,256,8192]{2,1,0:T(8,128)(2,1)} %all-gather.6.cloned.1.call-done, bf16[8192,128]{1,0:T(8,128)(2,1)} %param.7, bf16[1,256,128]{2,1,0:T(8,128)(2,1)S(1)} %copy-done.5, f32[256]{0:T(256)S(1)} %bitcast.100), kind=kOutput, calls=%fused_computation.1 | convolution fusion | flops 1073971200 | bytes 10552320 | tf_op jit(solution)/shard_map/dot_general | solution.py:26
  129.2 0.0 copy-start
  129.2 0.0 copy-start.1
  129.2 0.0 copy-start.2
  129.2 0.0 copy-start.3
  129.2 10.3 %fusion.55 = bf16[256,128]{1,0:T(8,128)(2,1)S(1)} fusion(bf16[1,256,8192]{2,1,0:T(8,128)(2,1)} %all-gather.6.cloned.1.call-done, bf16[8192,128]{0,1:T(8,128)(2,1)S(1)} %copy.15, f32[8192,128]{0,1:T(8,128)} %convolution_bitcast_fusion.1, f32[1,8192,128]{1,2,0:T(8,128)} %copy.16, f32[1,8192,128]{1,2,0:T(8,128)} %copy.17, ...), kind=kOutput, calls=%fused_computation.30 | convolution fusion | flops 552828928 | bytes 19006464 | tf_op jit(solution)/shard_map/dot_general | solution.py:23
  139.5 0.0 copy-done
  139.5 0.0 copy-done.1
  139.5 0.0 copy-done.2
  139.5 0.3 copy-done.3
  139.9 8.1 %fusion.8 = f32[8192,128]{0,1:T(8,128)} fusion(bf16[256,128]{1,0:T(8,128)(2,1)S(1)} %fusion.55, bf16[1,256,8192]{2,1,0:T(8,128)(2,1)S(1)} %copy-done, bf16[8192,128]{0,1:T(8,128)(2,1)S(1)} %copy.15, f32[8192,128]{0,1:T(8,128)S(1)} %copy-done.3, f32[1,8192,128]{1,2,0:T(8,128)S(1)} %copy-done.1, f32[1,8192,128]{1,2,0:T(8,128)S(1)} %copy-done.2), kind=kOutput, calls=%fused_computation.12 | convolution fusion | flops 566231040 | bytes 23134208 | tf_op jit(solution)/shard_map/dot_general | solution.py:26
  147.9 0.0 reduce-scatter.2.cloned.1.call-update
  147.9 0.0 copy-start.4
  148.0 0.0 all-gather.4.cloned.1.call-start
  148.0 2.4 convert_element_type.37
  150.4 0.0 copy-done.4
  150.4 0.1 copy.18
  150.5 137.9 %reduce-scatter.2.cloned.1.call-done = f32[256,128]{0,1:T(8,128)} async-done(((f32[8192,128]{0,1:T(8,128)}), f32[256,128]{0,1:T(8,128)}) %reduce-scatter.2.cloned.1.call-update) | async-done | bytes 131088 | tf_op jit(solution)/shard_map/reduce_scatter | solution.py:35
  288.4 1.6 multiply_add_fusion
  290.1 0.0 all-gather.4.cloned.1.call-update
  290.1 0.8 copy.20
  290.8 65.8 %all-gather.4.cloned.1.call-done = bf16[8192,128]{0,1:T(8,128)(2,1)} async-done(((bf16[256,128]{0,1:T(8,128)(2,1)}), bf16[8192,128]{0,1:T(8,128)(2,1)}) %all-gather.4.cloned.1.call-update) | async-done | bytes 2097168 | tf_op jit(solution)/shard_map/all_gather | solution.py:40
  356.6 4.1 %copy.19 = bf16[8192,128]{1,0:T(8,128)(2,1)} copy(bf16[8192,128]{0,1:T(8,128)(2,1)} %all-gather.4.cloned.1.call-done) | data formatting | bytes 4194304
  (1 shorter events, 0.0 us)
Async XLA Ops:
  7.2 114.0 %all-gather.6.cloned.1.call-start = ((), (), s32[]{:S(2)}) async-start(), calls=%async_computation.3 | async-start | bytes 4718592 | tf_op jit(solution)/shard_map/all_gather | solution.py:12
  7.9 280.5 %reduce-scatter.2.cloned.1.call-start = ((), (), s32[]{:S(2)}) async-start(), calls=%async_computation.1 | async-start | bytes 4325376 | tf_op jit(solution)/shard_map/reduce_scatter | solution.py:35
  16.5 5.7 %copy-start.6 = (s32[1,2,512]{2,1,0:T(2,128)S(1)}, s32[1,2,512]{2,1,0:T(2,128)}, u32[]{:S(2)}) copy-start(s32[1,2,512]{2,1,0:T(2,128)} %param.13) | copy-start | bytes 12292
  16.5 104.7 %copy-start.5 = (bf16[1,256,128]{2,1,0:T(8,128)(2,1)S(1)}, bf16[1,256,128]{2,1,0:T(8,128)(2,1)}, u32[]{:S(2)}) copy-start(bf16[1,256,128]{2,1,0:T(8,128)(2,1)} %param.12) | copy-start | bytes 196612
  129.2 10.3 %copy-start = (bf16[1,256,8192]{2,1,0:T(8,128)(2,1)S(1)}, bf16[1,256,8192]{2,1,0:T(8,128)(2,1)}, u32[]{:S(2)}) copy-start(bf16[1,256,8192]{2,1,0:T(8,128)(2,1)} %all-gather.6.cloned.1.call-done) | copy-start | bytes 12582916
  129.2 10.3 %copy-start.1 = (f32[1,8192,128]{1,2,0:T(8,128)S(1)}, f32[1,8192,128]{1,2,0:T(8,128)}, u32[]{:S(2)}) copy-start(f32[1,8192,128]{1,2,0:T(8,128)} %copy.16) | copy-start | bytes 12582916
  129.2 10.3 %copy-start.2 = (f32[1,8192,128]{1,2,0:T(8,128)S(1)}, f32[1,8192,128]{1,2,0:T(8,128)}, u32[]{:S(2)}) copy-start(f32[1,8192,128]{1,2,0:T(8,128)} %copy.17) | copy-start | bytes 12582916
  129.2 10.7 %copy-start.3 = (f32[8192,128]{0,1:T(8,128)S(1)}, f32[8192,128]{0,1:T(8,128)}, u32[]{:S(2)}) copy-start(f32[8192,128]{0,1:T(8,128)} %convolution_bitcast_fusion.1) | copy-start | bytes 12582916
  147.9 2.4 copy-start.4
  148.0 208.7 %all-gather.4.cloned.1.call-start = ((), (), s32[]{:S(2)}) async-start(), calls=%async_computation.2 | async-start | bytes 2162688 | tf_op jit(solution)/shard_map/all_gather | solution.py:40
Sparse Core Ops, SparseCore 0:
  10.6 110.5 all-gather.5
  148.1 140.3 reduce-scatter.1
  290.8 65.8 all-gather.3

commit v2 on v1

v2 whole, which is shorter than its diff:
```python
import jax
import jax.numpy as jnp
from jax import lax
from jax.experimental import pallas as pl
from jax.experimental.pallas import tpu as pltpu
from jax.sharding import PartitionSpec as P

F32 = jnp.float32
BF16 = jnp.bfloat16
MESH = pl.DeviceIdType.MESH

Z_LO, Z_HI, X, Y, CORES = 4, 2, 4, 4, 2

CHUNKS = 4
STEP_ROWS = 512
ORDER = (2, 1, 3, 0)


def round_kernel(
    weights_hbm, momentum_ref, first_hbm, second_hbm, bank_hbm, target_ref, ids_ref,
    out_weights, out_momentum,
    bank, bank_t, relay, w0, w1, first, second, count, acc, scaled,
    pair_send, pair_recv, own_sum, far_send, far_recv, near_send, near_recv,
    line_send, line_recv, total, gathered,
    send_sems, recv_sems, local_sems,
):
    rep, fsdp = lax.axis_index("rep"), lax.axis_index("fsdp")
    core = rep % CORES
    x = (rep // CORES) % X
    z_lo = rep // (CORES * X)
    z_hi = fsdp % Z_HI
    y = fsdp // Z_HI
    depth = Z_LO * Z_HI
    z = z_hi * Z_LO + z_lo

    def device(x_at, y_at, z_at, core_at):
        return (((z_at % Z_LO) * X + x_at) * CORES + core_at, y_at * Z_HI + z_at // Z_LO)

    def line(distance):
        return z_hi * Z_LO + (z_lo + distance) % Z_LO

    y_up, y_down = device(x, (y + 1) % Y, z, core), device(x, (y + Y - 1) % Y, z, core)
    z_up, z_down = device(x, y, (z + 2) % depth, core), device(x, y, (z + depth - 2) % depth, core)
    x_up, x_down = device((x + 1) % X, y, z, core), device((x + X - 1) % X, y, z, core)
    pair = device(x, y, z, 1 - core)
    line_peers = {d: device(x, y, line(d), core) for d in (1, 2, 3)}

    barrier = pltpu.get_barrier_semaphore()
    peers = [y_up, y_down, z_up, z_down, x_up, x_down, pair] + [line_peers[d] for d in (1, 2, 3)]
    for peer in peers:
        pl.semaphore_signal(barrier, inc=1, device_id=peer, device_id_type=MESH)
    pl.semaphore_wait(barrier, len(peers))

    sent = []
    placed = []

    def send(src, dst, peer):
        at = len(sent)
        copy = pltpu.make_async_remote_copy(
            src_ref=src, dst_ref=dst, send_sem=send_sems.at[at], recv_sem=recv_sems.at[at],
            device_id=peer, device_id_type=MESH,
        )
        copy.start()
        sent.append(copy)
        return copy

    def place(src, dst):
        copy = pltpu.make_async_copy(src, dst, local_sems.at[len(placed)])
        copy.start()
        placed.append(copy)
        return copy

    rows_all, columns_all = bank.shape
    block = bank_hbm.shape[1]
    half = block // 2
    wide = columns_all // CHUNKS

    def part(slot, q, which=None):
        cols = pl.ds(q * wide, wide)
        if which is None:
            return bank.at[pl.ds(slot * block, block), cols]
        return bank.at[pl.ds(slot * block + which * half, half), cols]

    def own_part(q, which=None):
        cols = pl.ds(q * wide, wide)
        if which is None:
            return bank_hbm.at[0, :, cols]
        return bank_hbm.at[0, pl.ds(which * half, half), cols]

    def relay_part(q, which):
        return relay.at[which, :, pl.ds(q * wide, wide)]

    def z_first(q):
        return (send(own_part(q, 0), relay_part(q, 0), z_up),
                send(own_part(q, 1), relay_part(q, 1), z_down))

    z_own = {0: z_first(0)}
    y_own = {}
    for q in range(CHUNKS):
        y_own[q] = (send(own_part(q), part(1, q), y_up), send(own_part(q), part(2, q), y_down))
        if q == 0:
            z_own[1] = z_first(1)
    own_here = place(bank_hbm.at[0], bank.at[pl.ds(0, block), :])
    states_here = [
        place(weights_hbm, w0), place(first_hbm.at[0], first), place(second_hbm.at[0], second)
    ]

    inner_count, token_count = ids_ref.shape[1], ids_ref.shape[2]
    starts = []
    for z_of in (z_hi, 1 - z_hi):
        for y_of in (y, (y + Y - 1) % Y, (y + 1) % Y, (y + 2) % Y):
            starts.append(pl.multiple_of((y_of * Z_HI + z_of) * block, block))
    for k in range(inner_count):
        ids = jnp.broadcast_to(ids_ref[0, k:k + 1, :], (block, token_count))
        for slot, start in enumerate(starts):
            row = lax.broadcasted_iota(jnp.int32, (block, token_count), 0) + start
            hits = jnp.where(ids == row, 1.0, 0.0).astype(F32)
            number = jnp.sum(hits, axis=1, keepdims=True)
            count[k, pl.ds(slot * block, block), :] = jnp.broadcast_to(number, (block, 128))

    z_relayed, y_passed, y_partner, partner_passed = {}, {}, {}, {}
    for q in range(CHUNKS):
        for copy in z_own[q]:
            copy.wait_recv()
        z_relayed[q] = (send(relay_part(q, 0), part(4, q, 0), z_up),
                        send(relay_part(q, 1), part(4, q, 1), z_down))
        if q + 2 < CHUNKS:
            z_own[q + 2] = z_first(q + 2)
        for copy in y_own[q]:
            copy.wait_recv()
        y_passed[q] = (send(part(1, q, 0), part(3, q, 0), y_up),
                       send(part(2, q, 1), part(3, q, 1), y_down))

    def partner_on(q):
        for copy in z_relayed[q]:
            copy.wait_recv()
        y_partner[q] = (send(part(4, q), part(5, q), y_up), send(part(4, q), part(6, q), y_down))

    def partner_pass(q):
        for copy in y_partner[q]:
            copy.wait_recv()
        partner_passed[q] = (send(part(5, q, 0), part(7, q, 0), y_up),
                             send(part(6, q, 1), part(7, q, 1), y_down))

    group = rows_all // 2

    def first_product(g, q):
        rows = pl.ds(g * group, group)

        def body(i, unused):
            cols = pl.ds(pl.multiple_of(q * wide + i * 512, 512), 512)
            tile = bank[rows, cols]
            acc[rows, :] += jnp.dot(tile, w0[cols, :], preferred_element_type=F32)
            bank_t[cols, rows] = tile.T
            return unused

        lax.fori_loop(0, wide // 512, body, 0)

    acc[...] = jnp.zeros_like(acc)
    partner_on(0)
    partner_on(1)
    own_here.wait()
    for copy in states_here:
        copy.wait()
    for q in range(CHUNKS):
        for copy in y_passed[q]:
            copy.wait_recv()
        first_product(0, q)
        if q + 2 < CHUNKS:
            partner_on(q + 2)
        else:
            partner_pass(q + 2 - CHUNKS)
    for q in range(2, CHUNKS):
        partner_pass(q)
    for q in range(CHUNKS):
        for copy in partner_passed[q]:
            copy.wait_recv()
        first_product(1, q)

    def weigh(k):
        for slot, start in enumerate(starts):
            rows = pl.ds(slot * block, block)
            wanted = target_ref[0, pl.ds(start, block), :].astype(F32)
            residual = ((acc[rows, :] - wanted) / token_count).astype(BF16).astype(F32)
            scaled[rows, :] = (residual * count[k, rows, :]).astype(BF16)

    def moments(rows):
        gradient = jnp.dot(bank_t[rows, :], scaled[...], preferred_element_type=F32)
        m = 0.9 * first[rows, :] + 0.1 * gradient
        v = 0.95 * second[rows, :] + 0.05 * gradient * gradient
        return m, v

    def stepped(w, m, v):
        return w - 0.1 * (m / (jnp.sqrt(v) + 1e-08) + 0.1 * w)

    weigh(0)
    acc[...] = jnp.zeros_like(acc)

    def first_step(i, unused):
        rows = pl.ds(pl.multiple_of(i * STEP_ROWS, STEP_ROWS), STEP_ROWS)
        m, v = moments(rows)
        first[rows, :] = m
        second[rows, :] = v
        w = stepped(w0[rows, :].astype(F32), m, v)
        w1[rows, :] = w
        acc[...] += jnp.dot(bank[:, rows], w.astype(BF16), preferred_element_type=F32)
        return unused

    lax.fori_loop(0, columns_all // STEP_ROWS, first_step, 0)
    weigh(1)

    share = momentum_ref.shape[0]

    def change(x_dist, z_dist, core_at):
        row_block = (((z_lo + z_dist) % Z_LO) * X + (x + x_dist) % X) * CORES + core_at
        rows = pl.ds(pl.multiple_of(row_block * share, share), share)
        m, v = moments(rows)
        return w0[rows, :].astype(F32) - stepped(w1[rows, :], m, v)

    pair_copies = {}

    def for_pair(x_dist):
        def body(z_dist, unused):
            pair_send[x_dist, z_dist] = change(x_dist, z_dist, 1 - core).astype(BF16)
            return unused

        lax.fori_loop(0, Z_LO, body, 0)
        pair_copies[x_dist] = send(pair_send.at[x_dist], pair_recv.at[x_dist], pair)

    def for_own(x_dist):
        pair_copies[x_dist].wait_recv()

        def body(z_dist, unused):
            both = change(x_dist, z_dist, core) + pair_recv[x_dist, z_dist].astype(F32)
            if x_dist == 2:
                far_send[z_dist] = both.astype(BF16)
            else:
                own_sum[x_dist, z_dist] = both
            return unused

        lax.fori_loop(0, Z_LO, body, 0)

    mid = share // 2
    low, high = pl.ds(0, mid), pl.ds(mid, mid)
    far_copies, near_up, near_down = {}, {}, {}

    def pass_up(z_dist):
        far_copies[z_dist][0].wait_recv()
        near_send[0, z_dist, low, :] = (
            own_sum[1, z_dist, low, :] + far_recv[0, z_dist].astype(F32)
        ).astype(BF16)
        near_send[0, z_dist, high, :] = own_sum[1, z_dist, high, :].astype(BF16)
        near_up[z_dist] = send(near_send.at[0, z_dist], near_recv.at[0, z_dist], x_up)

    def pass_down(z_dist):
        far_copies[z_dist][1].wait_recv()
        near_send[1, z_dist, high, :] = (
            own_sum[3, z_dist, high, :] + far_recv[1, z_dist].astype(F32)
        ).astype(BF16)
        near_send[1, z_dist, low, :] = own_sum[3, z_dist, low, :].astype(BF16)
        near_down[z_dist] = send(near_send.at[1, z_dist], near_recv.at[1, z_dist], x_down)

    for_pair(2)
    for_pair(1)
    for_own(2)
    for d in ORDER:
        far_copies[d] = (send(far_send.at[d, low], far_recv.at[0, d], x_up),
                         send(far_send.at[d, high], far_recv.at[1, d], x_down))
    for_pair(3)
    for_own(1)
    for_pair(0)
    for_own(3)
    for d in ORDER:
        pass_up(d)
        pass_down(d)
    for_own(0)

    line_copies = {}
    for d in ORDER:
        near_up[d].wait_recv()
        near_down[d].wait_recv()
        summed = (
            own_sum[0, d] + near_recv[0, d].astype(F32) + near_recv[1, d].astype(F32)
        )
        if d:
            line_send[d - 1] = summed.astype(BF16)
            line_copies[d] = send(line_send.at[d - 1], line_recv.at[d - 1], line_peers[d])
        else:
            total[...] = summed
    for d in (1, 3, 2):
        line_copies[d].wait_recv()
    average = (
        total[...] + line_recv[0].astype(F32) + line_recv[1].astype(F32) + line_recv[2].astype(F32)
    ) / (Z_LO * X * CORES)
    new_momentum = 0.9 * momentum_ref[...] + average
    out_momentum[...] = new_momentum
    own_rows = pl.ds(pl.multiple_of(rep * share, share), share)
    start_share = w0[own_rows, :].astype(F32)
    gathered[z_lo, x] = (start_share - 0.7 * (average + 0.9 * new_momentum)).astype(BF16)

    pair_got = []

    def z_from(d):
        return (z_lo + Z_LO - d) % Z_LO

    def keep(d, x_dist):
        z_at, x_at = z_from(d), (x + x_dist) % X
        at = ((z_at * X + x_at) * CORES + core) * share
        out = out_weights.at[pl.ds(pl.multiple_of(at, share), share), :]
        here = gathered.at[z_at, x_at]
        place(here, out)
        pair_got.append(send(here, out, pair))

    def round_x(d):
        here = gathered.at[z_from(d), x]
        return send(here, here, x_up), send(here, here, x_down)

    def onward(d):
        up, down = round_copies[d]
        up.wait_recv()
        here = gathered.at[z_from(d), (x + X - 1) % X, low]
        above = send(here, here, x_up)
        down.wait_recv()
        here = gathered.at[z_from(d), (x + 1) % X, high]
        below = send(here, here, x_down)
        keep(d, X - 1)
        keep(d, 1)
        return above, below

    own_block = gathered.at[z_lo, x]
    line_got = {d: send(own_block, own_block, line_peers[d]) for d in (1, 3, 2)}
    round_copies = {0: round_x(0)}
    keep(0, 0)
    onward_copies = {}
    for d in (1, 3, 2):
        line_got[d].wait_recv()
        round_copies[d] = round_x(d)
        keep(d, 0)
        previous = {1: 0, 3: 1, 2: 3}[d]
        onward_copies[previous] = onward(previous)
    onward_copies[2] = onward(2)
    for d in (0, 1, 3, 2):
        for copy in onward_copies[d]:
            copy.wait_recv()
        keep(d, 2)

    for copy in pair_got:
        copy.wait_recv()
    for copy in sent:
        copy.wait_send()
    for copy in placed[4:]:
        copy.wait()


def per_device(
    global_weights, momentum, first_moment, second_moment, hidden_bank, target_bank, token_ids
):
    depth, width = global_weights.shape
    block = hidden_bank.shape[1]
    store = target_bank.shape[1]
    inner_count = token_ids.shape[1]
    share = momentum.shape[0]
    anywhere = pl.BlockSpec(memory_space=pl.ANY)
    inside = pl.BlockSpec(memory_space=pltpu.VMEM)
    vmem = pltpu.VMEM
    return pl.pallas_call(
        round_kernel,
        out_shape=(
            jax.ShapeDtypeStruct((depth, width), BF16),
            jax.ShapeDtypeStruct((share, width), F32),
        ),
        in_specs=[anywhere, inside, anywhere, anywhere, anywhere, inside, inside],
        out_specs=(anywhere, inside),
        scratch_shapes=[
            vmem((store, depth), BF16),
            vmem((depth, store), BF16),
            vmem((2, block // 2, depth), BF16),
            vmem((depth, width), BF16),
            vmem((depth, width), F32),
            vmem((depth, width), F32),
            vmem((depth, width), F32),
            vmem((inner_count, store, width), F32),
            vmem((store, width), F32),
            vmem((store, width), BF16),
            vmem((X, Z_LO, share, width), BF16),
            vmem((X, Z_LO, share, width), BF16),
            vmem((X, Z_LO, share, width), F32),
            vmem((Z_LO, share, width), BF16),
            vmem((2, Z_LO, share // 2, width), BF16),
            vmem((2, Z_LO, share, width), BF16),
            vmem((2, Z_LO, share, width), BF16),
            vmem((Z_LO - 1, share, width), BF16),
            vmem((Z_LO - 1, share, width), BF16),
            vmem((share, width), F32),
            vmem((Z_LO, X, share, width), BF16),
            pltpu.SemaphoreType.DMA((112,)),
            pltpu.SemaphoreType.DMA((112,)),
            pltpu.SemaphoreType.DMA((24,)),
        ],
        compiler_params=pltpu.CompilerParams(
            collective_id=0, has_side_effects=True, vmem_limit_bytes=60 * 1024 * 1024
        ),
        name="diloco_round",
    )(
        global_weights, momentum, first_moment, second_moment, hidden_bank, target_bank, token_ids
    )


def solution(mesh):
    return jax.shard_map(
        per_device,
        mesh=mesh,
        in_specs=(
            P(None, "fsdp"),
            P("rep", "fsdp"),
            P("rep", None, "fsdp"),
            P("rep", None, "fsdp"),
            P("rep", "fsdp", None),
            P("rep", None, "fsdp"),
            P("rep", None, None),
        ),
        out_specs=(P(None, "fsdp"), P("rep", "fsdp")),
        check_vma=False,
    )
```

time: 368 us -> 104 us (0.28)
  waiting for transfers between devices: 303 us -> 0 us
  Pallas kernels: 0 us -> 99 us
  matrix products: 26.3 us -> 0 us
  local copies, waits for them, and re-layouts: 19.5 us -> 3.74 us
  between operations: 13.8 us -> 0.65 us
  other arithmetic: 4.2 us -> 0 us
    all_gather x2 -> x0, waiting for transfers between devices: 165 us -> none  [the longest x1 98.8 us: per_device(): bank = lax.all_gather(hidden_bank[0], 'fsdp', axis=0, tiled=True)]
    reduce_scatter x1 -> x0, waiting for transfers between devices: 138 us -> none  [per_device(): lax.psum_scatter(local_change, 'rep', scatter_dimension=0, tiled=True)]
    pallas_call x0 -> x1, Pallas kernels: none -> 99 us  [per_device(): pl.pallas_call(round_kernel, out_shape=(jax.ShapeDtypeStruct((depth, widt...]
    dot_general x3 -> x0, matrix products: 26.3 us -> none  [the longest x2 16 us: per_device(): lax.dot_general(bank, scaled, (((0,), (0,)), ((), ())), preferred_element...]
    unnamed x20 -> x4, local copies, waits for them, and re-layouts: 19.5 us -> 3.74 us
  transfers between devices with their start and end apart: 3 -> 0, of which waited for: 3 -> 0; matrix products, arithmetic and copies ran while one was open for 5% -> 0% of each run, Pallas kernels for 0% -> 0%
where the time goes in v2:
time: 104 us; the launch traced here: 103 us
  Pallas kernels  99 us (95%)
  local copies, waits for them, and re-layouts  3.74 us (4%)
    pallas_call x1, Pallas kernels, per_device(): pl.pallas_call(round_kernel, out_shape=(jax.ShapeDtypeStruct((depth, widt...  99 us
    unnamed x4, local copies, waits for them, and re-layouts  3.74 us

profile of v2, /device:TPU:1, one launch (start us, length us, event | category | flops | bytes accessed | tf_op | source)
XLA Modules:
  0.0 103.4 jit_solution(5929630357113486473)
XLA Ops:
  0.6 99.0 %diloco_round.1 = (bf16[8192,128]{1,0:T(8,128)(2,1)}, f32[256,128]{1,0:T(8,128)}) custom-call(bf16[8192,128]{1,0:T(8,128)(2,1)} %weights_hbm.1, f32[256,128]{1,0:T(8,128)} %momentum_ref.1, f32[1,8192,128]{2,1,0:T(8,128)} %first_hbm.1, f32[1,8192,128]{2,1,0:T(8,128)} %second_hbm.1, bf16[1,32,8192]{2,1,0:T(8,128)(2,1)} %bank_hbm.1, ...), custom_call_target="tpu_custom_call" | custom-call | tf_op jit(solution)/shard_map/diloco_round/pallas_call | solution.py:366
  99.7 0.0 copy-start
  99.7 3.1 %copy.11 = bf16[8192,128]{1,0:T(8,128)(2,1)} copy(bf16[8192,128]{1,0:T(8,128)(2,1)} %get-tuple-element.4) | data formatting | bytes 4194304
  102.8 0.0 copy-done
  102.8 0.7 copy.12
Async XLA Ops:
  99.7 3.1 %copy-start = (f32[256,128]{1,0:T(8,128)S(1)}, f32[256,128]{1,0:T(8,128)}, u32[]{:S(2)}) copy-start(f32[256,128]{1,0:T(8,128)} %get-tuple-element.5) | copy-start | bytes 393220

commit v3 on v2

--- a/solution.py
+++ b/solution.py
@@ -21,7 +21,7 @@
     out_weights, out_momentum,
     bank, bank_t, relay, w0, w1, first, second, count, acc, scaled,
     pair_send, pair_recv, own_sum, far_send, far_recv, near_send, near_recv,
-    line_send, line_recv, total, gathered,
+    line_send, line_recv, total,
     send_sems, recv_sems, local_sems,
 ):
     rep, fsdp = lax.axis_index("rep"), lax.axis_index("fsdp")
@@ -119,13 +119,16 @@
             count[k, pl.ds(slot * block, block), :] = jnp.broadcast_to(number, (block, 128))
 
     z_relayed, y_passed, y_partner, partner_passed = {}, {}, {}, {}
-    for q in range(CHUNKS):
+
+    def relay_on(q):
         for copy in z_own[q]:
             copy.wait_recv()
         z_relayed[q] = (send(relay_part(q, 0), part(4, q, 0), z_up),
                         send(relay_part(q, 1), part(4, q, 1), z_down))
         if q + 2 < CHUNKS:
             z_own[q + 2] = z_first(q + 2)
+
+    def own_pass(q):
         for copy in y_own[q]:
             copy.wait_recv()
         y_passed[q] = (send(part(1, q, 0), part(3, q, 0), y_up),
@@ -144,7 +147,9 @@
 
     group = rows_all // 2
 
-    def first_product(g, q):
+    def product(g, q):
+        for copy in (y_passed, partner_passed)[g][q]:
+            copy.wait_recv()
         rows = pl.ds(g * group, group)
 
         def body(i, unused):
@@ -157,25 +162,32 @@
         lax.fori_loop(0, wide // 512, body, 0)
 
     acc[...] = jnp.zeros_like(acc)
+    relay_on(0)
+    own_pass(0)
+    own_pass(1)
+    relay_on(1)
+    own_pass(2)
     partner_on(0)
-    partner_on(1)
+    own_pass(3)
+    relay_on(2)
     own_here.wait()
     for copy in states_here:
         copy.wait()
-    for q in range(CHUNKS):
-        for copy in y_passed[q]:
-            copy.wait_recv()
-        first_product(0, q)
-        if q + 2 < CHUNKS:
-            partner_on(q + 2)
-        else:
-            partner_pass(q + 2 - CHUNKS)
-    for q in range(2, CHUNKS):
-        partner_pass(q)
-    for q in range(CHUNKS):
-        for copy in partner_passed[q]:
-            copy.wait_recv()
-        first_product(1, q)
+    product(0, 0)
+    partner_on(1)
+    product(0, 1)
+    relay_on(3)
+    partner_pass(0)
+    product(0, 2)
+    partner_on(2)
+    partner_pass(1)
+    product(0, 3)
+    partner_on(3)
+    partner_pass(2)
+    product(1, 0)
+    partner_pass(3)
+    for q in range(1, CHUNKS):
+        product(1, q)
 
     def weigh(k):
         for slot, start in enumerate(starts):
@@ -296,38 +308,36 @@
     out_momentum[...] = new_momentum
     own_rows = pl.ds(pl.multiple_of(rep * share, share), share)
     start_share = w0[own_rows, :].astype(F32)
-    gathered[z_lo, x] = (start_share - 0.7 * (average + 0.9 * new_momentum)).astype(BF16)
+    out_weights[own_rows, :] = (start_share - 0.7 * (average + 0.9 * new_momentum)).astype(BF16)
 
     pair_got = []
 
-    def z_from(d):
-        return (z_lo + Z_LO - d) % Z_LO
+    def held(d, x_dist, start=0, size=share):
+        z_at, x_at = (z_lo + Z_LO - d) % Z_LO, (x + x_dist) % X
+        at = ((z_at * X + x_at) * CORES + core) * share + start
+        return out_weights.at[pl.ds(pl.multiple_of(at, mid), size), :]
 
     def keep(d, x_dist):
-        z_at, x_at = z_from(d), (x + x_dist) % X
-        at = ((z_at * X + x_at) * CORES + core) * share
-        out = out_weights.at[pl.ds(pl.multiple_of(at, share), share), :]
-        here = gathered.at[z_at, x_at]
-        place(here, out)
-        pair_got.append(send(here, out, pair))
+        here = held(d, x_dist)
+        pair_got.append(send(here, here, pair))
 
     def round_x(d):
-        here = gathered.at[z_from(d), x]
+        here = held(d, 0)
         return send(here, here, x_up), send(here, here, x_down)
 
     def onward(d):
         up, down = round_copies[d]
         up.wait_recv()
-        here = gathered.at[z_from(d), (x + X - 1) % X, low]
+        here = held(d, X - 1, 0, mid)
         above = send(here, here, x_up)
         down.wait_recv()
-        here = gathered.at[z_from(d), (x + 1) % X, high]
+        here = held(d, 1, mid, mid)
         below = send(here, here, x_down)
         keep(d, X - 1)
         keep(d, 1)
         return above, below
 
-    own_block = gathered.at[z_lo, x]
+    own_block = held(0, 0)
     line_got = {d: send(own_block, own_block, line_peers[d]) for d in (1, 3, 2)}
     round_copies = {0: round_x(0)}
     keep(0, 0)
@@ -348,8 +358,6 @@
         copy.wait_recv()
     for copy in sent:
         copy.wait_send()
-    for copy in placed[4:]:
-        copy.wait()
 
 
 def per_device(
@@ -366,11 +374,11 @@
     return pl.pallas_call(
         round_kernel,
         out_shape=(
-            jax.ShapeDtypeStruct((depth, width), BF16),
-            jax.ShapeDtypeStruct((share, width), F32),
+            vmem((depth, width), BF16),
+            vmem((share, width), F32),
         ),
         in_specs=[anywhere, inside, anywhere, anywhere, anywhere, inside, inside],
-        out_specs=(anywhere, inside),
+        out_specs=(inside, inside),
         scratch_shapes=[
             vmem((store, depth), BF16),
             vmem((depth, store), BF16),
@@ -392,10 +400,9 @@
             vmem((Z_LO - 1, share, width), BF16),
             vmem((Z_LO - 1, share, width), BF16),
             vmem((share, width), F32),
-            vmem((Z_LO, X, share, width), BF16),
             pltpu.SemaphoreType.DMA((112,)),
             pltpu.SemaphoreType.DMA((112,)),
-            pltpu.SemaphoreType.DMA((24,)),
+            pltpu.SemaphoreType.DMA((4,)),
         ],
         compiler_params=pltpu.CompilerParams(
             collective_id=0, has_side_effects=True, vmem_limit_bytes=60 * 1024 * 1024

time: 104 us -> 97.7 us (0.939)
  Pallas kernels: 99 us -> 95 us
  local copies, waits for them, and re-layouts: 3.74 us -> 1.98 us
    pallas_call x1, Pallas kernels: 99 us -> 95 us  [per_device(): pl.pallas_call(round_kernel, out_shape=(vmem((depth, width), BF16), vmem(...]
    unnamed x4 -> x2, local copies, waits for them, and re-layouts: 3.74 us -> 1.98 us
where the time goes in v3:
time: 97.7 us; the launch traced here: 97.6 us
  Pallas kernels  95 us (97%)
  local copies, waits for them, and re-layouts  1.98 us (2%)
    pallas_call x1, Pallas kernels, per_device(): pl.pallas_call(round_kernel, out_shape=(vmem((depth, width), BF16), vmem(...  95 us
    unnamed x2, local copies, waits for them, and re-layouts  1.98 us

profile of v3, /device:TPU:1, one launch (start us, length us, event | category | flops | bytes accessed | tf_op | source)
XLA Modules:
  0.0 97.6 jit_solution(14931207765806165092)
XLA Ops:
  0.6 95.0 %diloco_round.1 = (bf16[8192,128]{1,0:T(8,128)(2,1)S(1)}, f32[256,128]{1,0:T(8,128)S(1)}) custom-call(bf16[8192,128]{1,0:T(8,128)(2,1)} %weights_hbm.1, f32[256,128]{1,0:T(8,128)} %momentum_ref.1, f32[1,8192,128]{2,1,0:T(8,128)} %first_hbm.1, f32[1,8192,128]{2,1,0:T(8,128)} %second_hbm.1, bf16[1,32,8192]{2,1,0:T(8,128)(2,1)} %bank_hbm.1, ...), custom_call_target="tpu_custom_call" | custom-call | tf_op jit(solution)/shard_map/diloco_round/pallas_call | solution.py:374
  95.6 1.3 %copy.11 = bf16[8192,128]{1,0:T(8,128)(2,1)} copy(bf16[8192,128]{1,0:T(8,128)(2,1)S(1)} %get-tuple-element.2) | data formatting | bytes 4194304
  96.9 0.7 copy.12
